TPU v7x, 32 devices: a whole 2x2x4 slice. The times are simulated.
32 devices in a mesh: group: 4 (over x, core), fsdp: 8 (over z, y).
Axes of the slice: x: 2, y: 2, z: 4, core: 2. Of those that a mesh axis runs over, the one named last changes fastest.
Arguments:
- resid_in: bfloat16 [64, 320, 1536], P(('group', 'fsdp')), may hold values from -44 to 44
- attn_out: bfloat16 [64, 320, 1536], P(('group', 'fsdp')), may hold values from -6 to 6
- target_rows: bfloat16 [64, 320, 1536], P(('group', 'fsdp')), may hold values from -6 to 6
- out_weight: bfloat16 [1536, 1536], P('fsdp'), may hold values from -0.15625 to 0.15625
- norm_gain: bfloat16 [1536], replicated, may hold values from 0.099609375 to 1.8984375
- seq_lengths: int32 [64], replicated, may hold values from 33 to 320, as said below
- prompt_ids: int32 [64], replicated, may hold values from 0 to 31, as said below
- log_offsets: float32 [64], replicated, may hold values from -48 to 57
- plan_dest: int32 [64, 5], replicated, may hold values from -1 to 3, as said below
- plan_slot: int32 [64, 5], replicated, may hold values from -1 to 5, as said below
Outputs:
- resid_grad: bfloat16 [64, 320, 1536], P(('group', 'fsdp'))
- attn_grad: bfloat16 [64, 320, 1536], P(('group', 'fsdp'))
- weight_grad: float32 [1536, 1536], P('fsdp')
- loss: float32 [], replicated
Inputs may be any that keep to these rules, and one draw needn't show every extreme that they name: `seq_lengths`: A sequence of length l covers its first ceil(l / 64) buckets; the sequences of one index of fsdp cover exactly 24 buckets together, and on every index of fsdp some device has all 2 sequences of length 320. `plan_dest`: -1 exactly for buckets that the sequence doesn't cover. Among the devices of one index of fsdp, each works on exactly 6 buckets, and no device sends more than 3 of its buckets to one device; some device sends exactly 3 to one device. `plan_slot`: -1 where plan_dest is -1. For one index of fsdp, every pair of working device and position below 6 is taken by exactly one bucket. `prompt_ids`: the sequences of index g along group (g * 2 * 8 onwards) belong to prompts g * 8 to g * 8 + 7, each prompt with exactly 2 sequences.
All inputs are finite; a program needn't handle non-finite values.
Results may differ from a plain program's by a relative error of at most 0.005.
Values may be sent and summed in bfloat16 or wider, within the bound.
No kernel may reach another device: no remote copies, remote signals or barrier semaphores. Data moves between devices by JAX's collectives and lax.ppermute only.
A program may use at most 128 MiB of HBM per device.

v0:
```python
import math
import jax
import jax.numpy as jnp
from jax import lax
from jax.sharding import PartitionSpec as P

PPG = 8
EPS = 1e-06


def forward_rows(x_rows, o_rows, e_rows, weight, gain, mask):
    width = x_rows.shape[-1]
    mixed = x_rows.astype(jnp.float32) + jnp.dot(o_rows, weight, preferred_element_type=jnp.float32)
    scale_inv = lax.rsqrt(jnp.mean(mixed * mixed, axis=-1, keepdims=True) + EPS)
    normed = mixed * scale_inv * gain.astype(jnp.float32)
    token_logp = jnp.sum(normed * e_rows.astype(jnp.float32), axis=-1) * mask / math.sqrt(width)
    return (mixed, scale_inv, token_logp)


def backward_rows(mixed, scale_inv, e_rows, gain, coeff, weight):
    width = mixed.shape[-1]
    gained = (
        coeff[:, None] * e_rows.astype(jnp.float32) * gain.astype(jnp.float32) / math.sqrt(width)
    )
    inner = jnp.mean(mixed * gained, axis=-1, keepdims=True)
    grad_rows = (scale_inv * gained - mixed * scale_inv**3 * inner).astype(jnp.bfloat16)
    attn_rows = lax.dot_general(
        grad_rows, weight, (((1,), (1,)), ((), ())), preferred_element_type=jnp.float32
    ).astype(jnp.bfloat16)
    return (grad_rows, attn_rows)


def local(
    resid_in,
    attn_out,
    target_rows,
    out_weight,
    norm_gain,
    seq_lengths,
    prompt_ids,
    log_offsets,
    plan_dest,
    plan_slot,
):
    seq_dev, lmax, width = resid_in.shape
    n_group = lax.axis_size("group")
    n_fsdp = lax.axis_size("fsdp")
    group_idx = lax.axis_index("group")
    fsdp_idx = lax.axis_index("fsdp")
    total_seqs = seq_lengths.shape[0]
    prompts = PPG * n_group
    samples = seq_dev * n_fsdp // PPG
    prompt_range = jnp.arange(prompts, dtype=jnp.int32)
    weight = lax.all_gather(out_weight, "fsdp", axis=0, tiled=True)
    first = (group_idx * n_fsdp + fsdp_idx) * seq_dev
    my_len = lax.dynamic_slice_in_dim(seq_lengths, first, seq_dev)
    positions = jnp.arange(lmax, dtype=jnp.int32)
    mask = (positions[None, :] < my_len[:, None]).astype(jnp.float32).reshape(-1)
    x_rows = resid_in.reshape(-1, width)
    o_rows = attn_out.reshape(-1, width)
    e_rows = target_rows.reshape(-1, width)
    mixed, scale_inv, token_logp = forward_rows(x_rows, o_rows, e_rows, weight, norm_gain, mask)
    seq_logp = jnp.sum(token_logp.reshape(seq_dev, lmax), axis=1)
    delta = seq_logp + lax.dynamic_slice_in_dim(log_offsets, first, seq_dev)
    my_prompt = lax.dynamic_slice_in_dim(prompt_ids, first, seq_dev)
    member = (my_prompt[:, None] == prompt_range[None, :]).astype(jnp.float32)
    prompt_part = jnp.sum(member * delta[:, None], axis=0)
    prompt_total = lax.psum(prompt_part, "fsdp")
    baseline = prompt_total / samples
    centred = delta - jnp.sum(member * baseline[None, :], axis=1)
    square_total = lax.psum(jnp.sum(centred * centred), ("group", "fsdp"))
    coeff = jnp.repeat(centred, lmax) * mask
    grad_rows, attn_rows = backward_rows(mixed, scale_inv, e_rows, norm_gain, coeff, weight)
    resid_grad = grad_rows.reshape(seq_dev, lmax, width)
    attn_grad = attn_rows.reshape(seq_dev, lmax, width)
    part_rows = lax.psum_scatter(
        lax.dot_general(
            o_rows, grad_rows, (((0,), (0,)), ((), ())), preferred_element_type=jnp.float32
        ),
        "fsdp",
        scatter_dimension=0,
        tiled=True,
    )
    weight_grad = lax.psum(part_rows, "group") / total_seqs
    loss = square_total / (total_seqs * lmax)
    return (resid_grad, attn_grad, weight_grad, loss)


def solution(mesh):
    return jax.shard_map(
        local,
        mesh=mesh,
        in_specs=(
            P(("group", "fsdp"), None, None),
            P(("group", "fsdp"), None, None),
            P(("group", "fsdp"), None, None),
            P("fsdp", None),
            P(),
            P(),
            P(),
            P(),
            P(),
            P(),
        ),
        out_specs=(
            P(("group", "fsdp"), None, None),
            P(("group", "fsdp"), None, None),
            P("fsdp", None),
            P(),
        ),
        check_vma=False,
    )
```

profile of v0, /device:TPU:0, one launch (start us, length us, event | category | flops | bytes accessed | tf_op | source)
XLA Modules:
  0.0 360.7 jit_solution(16981682612720377899)
XLA Ops:
  7.2 0.0 copy-start
  7.2 0.0 all-gather.2.cloned.1.call-start
  7.2 0.7 all-gather.2.cloned.1.call-update
  7.9 0.0 reduce-scatter.4.cloned.1.call-start
  8.0 0.7 dynamic_slice.9
  8.7 0.7 dynamic_slice.11
  9.4 0.7 convert_element_type.30
  10.1 82.1 %all-gather.2.cloned.1.call-done = bf16[1536,1536]{1,0:T(8,128)(2,1)} async-done(((bf16[192,1536]{1,0:T(8,128)(2,1)}), bf16[1536,1536]{1,0:T(8,128)(2,1)}) %all-gather.2.cloned.1.call-update) | async-done | bytes 4718608 | tf_op jit(solution)/shard_map/all_gather | solution.py:54
  92.3 0.0 copy-done
  92.3 0.0 copy-start.3
  92.3 6.4 %multiply_reduce_fusion = (f32[640]{0:T(1024)S(1)}, f32[640,1536]{1,0:T(8,128)S(1)}) fusion(bf16[640,1536]{1,0:T(8,128)(2,1)S(1)} %bitcast.19, bf16[1536,1536]{1,0:T(8,128)(2,1)} %all-gather.2.cloned.1.call-done, bf16[640,1536]{1,0:T(8,128)(2,1)} %bitcast.22), kind=kOutput, calls=%fused_computation.12 | convolution fusion | flops 3023830528 | bytes 12585472 | tf_op jit(solution)/shard_map/dot_general | solution.py:13
  98.7 0.0 copy-start.1
  98.7 0.0 copy-start.6
  98.7 1.8 copy-done.1
  100.6 0.0 copy-done.3
  100.6 0.8 fusion
  101.3 0.1 reduce_sum.67
  101.4 0.2 multiply_reduce_fusion.1
  101.6 0.0 copy-done.6
  101.6 0.1 dynamic-slice_add_fusion
  101.7 0.1 select_reduce_fusion.1
  101.8 18.8 %psum.21 = f32[32]{0:T(128)S(1)} all-reduce(f32[32]{0:T(128)S(1)} %select_reduce_fusion.1), channel_id=1, replica_groups=mesh['group'=4,'fsdp'=8] {'fsdp'}, use_global_device_ids=true, to_apply=%region_4.0 | all-reduce | flops 32 | bytes 256 | tf_op jit(solution)/shard_map/psum | solution.py:68
  120.6 0.2 select_reduce_fusion
  120.8 0.6 multiply_reduce_fusion.2
  121.4 0.1 fusion.8
  121.4 0.1 mul.116
  121.5 0.0 copy-start.2
  121.5 0.0 copy-start.4
  121.5 3.8 %fusion.7 = f32[640]{0:T(1024)S(1)} fusion(f32[640,1536]{1,0:T(8,128)} %copy-done.1, bf16[2,320,1536]{2,1,0:T(8,128)(2,1)} %param.12, f32[640]{0:T(1024)S(1)} %mul.116, f32[1536]{0:T(1024)S(1)} %convert_element_type.30), kind=kLoop, calls=%fused_computation.10 | loop fusion | flops 5897600 | bytes 5909504 | tf_op jit(solution)/shard_map/reduce_sum | solution.py:25
  125.3 0.1 copy-done.2
  125.4 0.6 copy-done.4
  126.0 1.2 fusion.5
  127.2 0.0 copy-start.5
  127.2 1.3 copy-done.5
  128.5 6.3 %convolution_bitcast_fusion = f32[1536,1536]{0,1:T(8,128)} fusion(bf16[640,1536]{1,0:T(8,128)(2,1)S(1)} %fusion.5, bf16[640,1536]{1,0:T(8,128)(2,1)S(1)} %bitcast.20), kind=kOutput, calls=%fused_computation | convolution fusion | flops 3019898880 | bytes 13369344 | tf_op jit(solution)/shard_map/dot_general | solution.py:77
  134.8 9.6 %copy.15 = f32[1536,1536]{1,0:T(8,128)} copy(f32[1536,1536]{0,1:T(8,128)} %convolution_bitcast_fusion) | data formatting | bytes 18874368
  144.4 0.0 reduce-scatter.4.cloned.1.call-update
  144.5 0.0 all-reduce.2.cloned.1.call-start
  144.5 41.5 %psum.23 = f32[]{:T(128)} all-reduce(f32[]{:T(128)} %get-tuple-element.16), channel_id=1, replica_groups=mesh['group'=4,'fsdp'=8] {'group','fsdp'}, use_global_device_ids=true, to_apply=%region_10.0 | all-reduce | flops 1 | bytes 8 | tf_op jit(solution)/shard_map/psum | solution.py:71
  186.6 118.4 %reduce-scatter.4.cloned.1.call-done = f32[192,1536]{1,0:T(8,128)} async-done(((f32[1536,1536]{1,0:T(8,128)}), f32[192,1536]{1,0:T(8,128)}) %reduce-scatter.4.cloned.1.call-update) | async-done | bytes 1179664
  305.0 2.9 copy.16
  307.9 0.0 all-reduce.2.cloned.1.call-update
  308.0 7.4 %convolution_convert_fusion = bf16[640,1536]{1,0:T(8,128)(2,1)} fusion(bf16[640,1536]{1,0:T(8,128)(2,1)} %copy-done.5, bf16[1536,1536]{1,0:T(8,128)(2,1)} %all-gather.2.cloned.1.call-done), kind=kOutput, calls=%fused_computation.13 | convolution fusion | flops 3020881920 | bytes 8650752 | tf_op jit(solution)/shard_map/dot_general | solution.py:27
  315.4 34.6 %all-reduce.2.cloned.1.call-done = f32[192,1536]{0,1:T(8,128)} async-done(((f32[192,1536]{0,1:T(8,128)}), f32[192,1536]{0,1:T(8,128)}) %all-reduce.2.cloned.1.call-update) | async-done | bytes 1179664 | tf_op jit(solution)/shard_map/psum | solution.py:84
  350.1 1.5 broadcast_multiply_fusion
  351.6 1.5 copy.14
  (3 shorter events, 0.0 us)
Async XLA Ops:
  7.2 85.1 %copy-start = (bf16[2,320,1536]{2,1,0:T(8,128)(2,1)S(1)}, bf16[2,320,1536]{2,1,0:T(8,128)(2,1)}, u32[]{:S(2)}) copy-start(bf16[2,320,1536]{2,1,0:T(8,128)(2,1)} %param.11) | copy-start | bytes 5898244
  7.2 85.1 %all-gather.2.cloned.1.call-start = ((), (), s32[]{:S(2)}) async-start(), calls=%async_computation.1 | async-start | bytes 5308416 | tf_op jit(solution)/shard_map/all_gather | solution.py:54
  7.9 297.1 %reduce-scatter.4.cloned.1.call-start = ((), (), s32[]{:S(2)}) async-start(), calls=%async_computation.3 | async-start | bytes 10616832
  92.3 8.3 %copy-start.3 = (bf16[2,320,1536]{2,1,0:T(8,128)(2,1)S(1)}, bf16[2,320,1536]{2,1,0:T(8,128)(2,1)}, u32[]{:S(2)}) copy-start(bf16[2,320,1536]{2,1,0:T(8,128)(2,1)} %param.12) | copy-start | bytes 5898244
  98.7 1.9 copy-start.1
  98.7 2.9 copy-start.6
  121.5 3.9 %copy-start.2 = (f32[640,1536]{1,0:T(8,128)S(1)}, f32[640,1536]{1,0:T(8,128)}, u32[]{:S(2)}) copy-start(f32[640,1536]{1,0:T(8,128)} %copy-done.1) | copy-start | bytes 11796484
  121.5 4.5 %copy-start.4 = (bf16[2,320,1536]{2,1,0:T(8,128)(2,1)S(1)}, bf16[2,320,1536]{2,1,0:T(8,128)(2,1)}, u32[]{:S(2)}) copy-start(bf16[2,320,1536]{2,1,0:T(8,128)(2,1)} %param.12) | copy-start | bytes 5898244
  127.2 1.3 copy-start.5
  144.5 205.6 %all-reduce.2.cloned.1.call-start = ((), (), s32[]{:S(2)}) async-start(), calls=%async_computation.2 | async-start | bytes 3145728 | tf_op jit(solution)/shard_map/psum | solution.py:84
Sparse Core Ops, SparseCore 0:
  10.2 82.0 all-gather.1
  144.6 160.4 reduce-scatter.3
  308.1 41.9 all-reduce.1
where the time goes:
time: 361 us
  waiting for transfers between devices  236 us (65%)
  blocking collectives  60.2 us (17%)
  matrix products  20.2 us (6%)
  local copies, waits for them, and re-layouts  19.4 us (5%)
  between operations  15.6 us (4%)
  other arithmetic  9.2 us (3%)
    unnamed x4, waiting for transfers between devices  119 us
    all_gather x1, waiting for transfers between devices, local(): weight = lax.all_gather(out_weight, 'fsdp', axis=0, tiled=True)  82.1 us
    psum x1, blocking collectives, local(): square_total = lax.psum(jnp.sum(centred * centred), ('group', 'fsdp'))  41.5 us
    psum x1, waiting for transfers between devices, local(): weight_grad = lax.psum(part_rows, 'group') / total_seqs  34.6 us
    psum x1, blocking collectives, local(): prompt_total = lax.psum(prompt_part, 'fsdp')  18.8 us
    unnamed x17, local copies, waits for them, and re-layouts  17.8 us
    dot_general x1, matrix products, backward_rows(): lax.dot_general(grad_rows, weight, (((1,), (1,)), ((), ())), preferred_el...  7.45 us
  transfers between devices with their start and end apart: 3, of which 3 were waited for; matrix products, arithmetic and copies ran while one was open for 3% of the time, Pallas kernels for 0%

commit v1 on v0

--- a/solution.py
+++ b/solution.py
@@ -81,7 +81,7 @@
         scatter_dimension=0,
         tiled=True,
     )
-    weight_grad = lax.psum(part_rows, "group") / total_seqs
+    weight_grad = jnp.sum(lax.all_gather(part_rows, "group"), axis=0) / total_seqs
     loss = square_total / (total_seqs * lmax)
     return (resid_grad, attn_grad, weight_grad, loss)
 

time: 361 us -> 364 us (level)
  waiting for transfers between devices: 236 us -> 242 us
  local copies, waits for them, and re-layouts: 19.4 us -> 15.1 us
    reduce_scatter x0 -> x1, waiting for transfers between devices: none -> 159 us  [local(): lax.psum_scatter(lax.dot_general(o_rows, grad_rows, (((0,), (0,)), ((), (...]
    unnamed x4 -> x3, waiting for transfers between devices: 119 us -> 0.71 us
    psum x1 -> x0, waiting for transfers between devices: 34.6 us -> none  [local(): weight_grad = lax.psum(part_rows, 'group') / total_seqs]
    unnamed x17 -> x15, local copies, waits for them, and re-layouts: 17.8 us -> 13.5 us
  transfers between devices with their start and end apart: 3 -> 3, of which waited for: 3 -> 2; matrix products, arithmetic and copies ran while one was open for 3% -> 3% of each run, Pallas kernels for 0% -> 0%
where the time goes in v1:
time: 364 us
  waiting for transfers between devices  242 us (66%)
  blocking collectives  58.9 us (16%)
  matrix products  20.2 us (6%)
  between operations  15.6 us (4%)
  local copies, waits for them, and re-layouts  15.1 us (4%)
  other arithmetic  11.7 us (3%)
    reduce_scatter x1, waiting for transfers between devices, local(): lax.psum_scatter(lax.dot_general(o_rows, grad_rows, (((0,), (0,)), ((), (...  159 us
    all_gather x1, waiting for transfers between devices, local(): weight = lax.all_gather(out_weight, 'fsdp', axis=0, tiled=True)  82.1 us
    psum x1, blocking collectives, local(): square_total = lax.psum(jnp.sum(centred * centred), ('group', 'fsdp'))  40.1 us
    psum x1, blocking collectives, local(): prompt_total = lax.psum(prompt_part, 'fsdp')  18.8 us
    unnamed x15, local copies, waits for them, and re-layouts  13.5 us
    dot_general x1, matrix products, backward_rows(): lax.dot_general(grad_rows, weight, (((1,), (1,)), ((), ())), preferred_el...  7.45 us
  transfers between devices with their start and end apart: 3, of which 2 were waited for; matrix products, arithmetic and copies ran while one was open for 3% of the time, Pallas kernels for 0%

profile of v1, /device:TPU:0, one launch (start us, length us, event | category | flops | bytes accessed | tf_op | source)
XLA Modules:
  0.0 363.9 jit_solution(13607536614219021242)
XLA Ops:
  7.2 0.0 copy-start
  7.2 0.0 all-gather.4.cloned.1.call-start
  7.2 0.7 all-gather.4.cloned.1.call-update
  7.9 0.0 reduce-scatter.4.cloned.1.call-start
  8.0 0.7 dynamic_slice.9
  8.7 0.7 dynamic_slice.11
  9.4 0.7 convert_element_type.30
  10.1 82.1 %all-gather.4.cloned.1.call-done = bf16[1536,1536]{1,0:T(8,128)(2,1)} async-done(((bf16[192,1536]{1,0:T(8,128)(2,1)}), bf16[1536,1536]{1,0:T(8,128)(2,1)}) %all-gather.4.cloned.1.call-update) | async-done | bytes 4718608 | tf_op jit(solution)/shard_map/all_gather | solution.py:54
  92.3 0.0 copy-done
  92.3 0.0 copy-start.3
  92.3 6.4 %multiply_reduce_fusion = (f32[640]{0:T(1024)S(1)}, f32[640,1536]{1,0:T(8,128)S(1)}) fusion(bf16[640,1536]{1,0:T(8,128)(2,1)S(1)} %bitcast.20, bf16[1536,1536]{1,0:T(8,128)(2,1)} %all-gather.4.cloned.1.call-done, bf16[640,1536]{1,0:T(8,128)(2,1)} %bitcast.24), kind=kOutput, calls=%fused_computation.12 | convolution fusion | flops 3023830528 | bytes 12585472 | tf_op jit(solution)/shard_map/dot_general | solution.py:13
  98.7 0.0 copy-start.1
  98.7 0.0 copy-start.6
  98.7 1.8 copy-done.1
  100.6 0.0 copy-done.3
  100.6 0.8 fusion
  101.3 0.1 reduce_sum.76
  101.4 0.2 multiply_reduce_fusion.1
  101.6 0.0 copy-done.6
  101.6 0.1 dynamic-slice_add_fusion
  101.7 0.1 select_reduce_fusion.1
  101.8 18.8 %psum.14 = f32[32]{0:T(128)S(1)} all-reduce(f32[32]{0:T(128)S(1)} %select_reduce_fusion.1), channel_id=1, replica_groups=mesh['group'=4,'fsdp'=8] {'fsdp'}, use_global_device_ids=true, to_apply=%region_4.0 | all-reduce | flops 32 | bytes 256 | tf_op jit(solution)/shard_map/psum | solution.py:68
  120.6 0.2 select_reduce_fusion
  120.8 0.6 multiply_reduce_fusion.2
  121.4 0.1 fusion.8
  121.4 0.1 mul.116
  121.5 0.0 copy-start.2
  121.5 0.0 copy-start.4
  121.5 3.8 %fusion.7 = f32[640]{0:T(1024)S(1)} fusion(f32[640,1536]{1,0:T(8,128)} %copy-done.1, bf16[2,320,1536]{2,1,0:T(8,128)(2,1)} %param.12, f32[640]{0:T(1024)S(1)} %mul.116, f32[1536]{0:T(1024)S(1)} %convert_element_type.30), kind=kLoop, calls=%fused_computation.10 | loop fusion | flops 5897600 | bytes 5909504 | tf_op jit(solution)/shard_map/reduce_sum | solution.py:25
  125.3 0.1 copy-done.2
  125.4 0.6 copy-done.4
  126.0 1.2 fusion.5
  127.2 0.0 copy-start.5
  127.2 1.3 copy-done.5
  128.5 6.3 %convolution_bitcast_fusion = f32[1536,1536]{0,1:T(8,128)} fusion(bf16[640,1536]{1,0:T(8,128)(2,1)S(1)} %fusion.5, bf16[640,1536]{1,0:T(8,128)(2,1)S(1)} %bitcast.21), kind=kOutput, calls=%fused_computation | convolution fusion | flops 3019898880 | bytes 13369344 | tf_op jit(solution)/shard_map/dot_general | solution.py:77
  134.8 9.6 %copy.15 = f32[1536,1536]{1,0:T(8,128)} copy(f32[1536,1536]{0,1:T(8,128)} %convolution_bitcast_fusion) | data formatting | bytes 18874368
  144.4 0.0 reduce-scatter.4.cloned.1.call-update
  144.5 0.0 all-gather.6.cloned.1.call-start
  144.5 159.5 %reduce-scatter.4.cloned.1.call-done = f32[192,1536]{1,0:T(8,128)} async-done(((f32[1536,1536]{1,0:T(8,128)}), f32[192,1536]{1,0:T(8,128)}) %reduce-scatter.4.cloned.1.call-update) | async-done | bytes 1179664 | tf_op jit(solution)/shard_map/reduce_scatter | solution.py:76
  304.0 0.0 all-gather.6.cloned.1.call-update
  304.0 40.1 %psum.15 = f32[]{:T(128)} all-reduce(f32[]{:T(128)} %get-tuple-element.4), channel_id=1, replica_groups=mesh['group'=4,'fsdp'=8] {'group','fsdp'}, use_global_device_ids=true, to_apply=%region_10.0 | all-reduce | flops 1 | bytes 8 | tf_op jit(solution)/shard_map/psum | solution.py:71
  344.8 7.5 %convolution_convert_fusion = bf16[640,1536]{1,0:T(8,128)(2,1)} fusion(bf16[640,1536]{1,0:T(8,128)(2,1)} %copy-done.5, bf16[1536,1536]{1,0:T(8,128)(2,1)} %all-gather.4.cloned.1.call-done), kind=kOutput, calls=%fused_computation.13 | convolution fusion | flops 3020881920 | bytes 8650752 | tf_op jit(solution)/shard_map/dot_general | solution.py:27
  352.3 0.0 all-gather.6.cloned.1.call-done
  352.3 2.9 reduce_sum.81
  355.2 1.1 broadcast_multiply_fusion
  (3 shorter events, 0.0 us)
Async XLA Ops:
  7.2 85.1 %copy-start = (bf16[2,320,1536]{2,1,0:T(8,128)(2,1)S(1)}, bf16[2,320,1536]{2,1,0:T(8,128)(2,1)}, u32[]{:S(2)}) copy-start(bf16[2,320,1536]{2,1,0:T(8,128)(2,1)} %param.11) | copy-start | bytes 5898244
  7.2 85.1 %all-gather.4.cloned.1.call-start = ((), (), s32[]{:S(2)}) async-start(), calls=%async_computation.1 | async-start | bytes 5308416 | tf_op jit(solution)/shard_map/all_gather | solution.py:54
  7.9 296.1 %reduce-scatter.4.cloned.1.call-start = ((), (), s32[]{:S(2)}) async-start(), calls=%async_computation.3 | async-start | bytes 10616832 | tf_op jit(solution)/shard_map/reduce_scatter | solution.py:76
  92.3 8.3 %copy-start.3 = (bf16[2,320,1536]{2,1,0:T(8,128)(2,1)S(1)}, bf16[2,320,1536]{2,1,0:T(8,128)(2,1)}, u32[]{:S(2)}) copy-start(bf16[2,320,1536]{2,1,0:T(8,128)(2,1)} %param.12) | copy-start | bytes 5898244
  98.7 1.9 copy-start.1
  98.7 2.9 copy-start.6
  121.5 3.9 %copy-start.2 = (f32[640,1536]{1,0:T(8,128)S(1)}, f32[640,1536]{1,0:T(8,128)}, u32[]{:S(2)}) copy-start(f32[640,1536]{1,0:T(8,128)} %copy-done.1) | copy-start | bytes 11796484
  121.5 4.5 %copy-start.4 = (bf16[2,320,1536]{2,1,0:T(8,128)(2,1)S(1)}, bf16[2,320,1536]{2,1,0:T(8,128)(2,1)}, u32[]{:S(2)}) copy-start(bf16[2,320,1536]{2,1,0:T(8,128)(2,1)} %param.12) | copy-start | bytes 5898244
  127.2 1.3 copy-start.5
  144.5 207.8 %all-gather.6.cloned.1.call-start = ((), (), s32[]{:S(2)}) async-start(), calls=%async_computation.2 | async-start | bytes 5898240 | tf_op jit(solution)/shard_map/all_gather | solution.py:84
Sparse Core Ops, SparseCore 0:
  10.2 82.0 all-gather.3
  144.6 159.3 reduce-scatter.3
  305.6 36.8 all-gather.5
